TPU v7x, 256 devices: a whole 4x4x8 slice. The times are simulated.
256 devices in a mesh: grp: 4 (over y), dev: 64 (over x, z, core).
Axes of the slice: x: 4, y: 4, z: 8, core: 2. Of those that a mesh axis runs over, the one named last changes fastest.
Arguments:
- field: float32 [512, 512, 256, 4], P('dev', 'grp'), may hold values from -21 to 21
- start_basis: float32 [512, 64], replicated, may hold values from -6 to 6
Outputs:
- factor: float32 [512, 64], replicated
- core: float32 [64, 512, 256, 4], P(None, ('grp', 'dev'))
All inputs are finite; a program needn't handle non-finite values.
Results may differ from a plain program's by a relative error of at most 0.0003.
Values sent between devices are 32-bit elements; how exact they have to be, the bound alone decides.
No kernel may reach another device: no remote copies, remote signals or barrier semaphores. Data moves between devices by JAX's collectives and lax.ppermute only.
A program may use at most 192 MiB of HBM per device.

v0:
```python
import jax
import jax.numpy as jnp
from jax import lax
from jax.sharding import PartitionSpec as P

ITERS = 3


def product(left, right):
    return jnp.dot(left, right, precision=lax.Precision.HIGHEST, preferred_element_type=jnp.float32)


def on_device(field, start_basis):
    regrouped = lax.all_to_all(field, "dev", split_axis=1, concat_axis=0, tiled=True)
    rows = regrouped.shape[0]
    local_cols = regrouped.shape[1] * regrouped.shape[2] * regrouped.shape[3]
    unfold = regrouped.reshape(rows, local_cols)
    local_gram = product(unfold, unfold.T)
    gram = lax.psum(local_gram, ("grp", "dev"))
    basis = start_basis
    for step in range(ITERS):
        image = product(gram, basis)
        cross = product(image.T, image)
        chol = jnp.linalg.cholesky(cross)
        basis = lax.linalg.triangular_solve(
            chol, image, left_side=False, lower=True, transpose_a=True
        )
    core = product(basis.T, unfold)
    return (
        basis,
        core.reshape(basis.shape[1], regrouped.shape[1], regrouped.shape[2], regrouped.shape[3]),
    )


def solution(mesh):
    placed = (P("dev", "grp", None, None), P())
    return jax.shard_map(
        on_device,
        mesh=mesh,
        in_specs=placed,
        out_specs=(P(), P(None, ("grp", "dev"), None, None)),
        check_vma=False,
    )
```

profile of v0, /device:TPU:2, one launch (start us, length us, event | category | flops | bytes accessed | tf_op | source)
XLA Modules:
  0.0 543.9 jit_solution(3584140676412488919)
XLA Ops:
  7.2 0.0 copy-start
  7.2 0.0 all-reduce.2.cloned.1.call-start
  7.2 3.4 copy.14
  10.7 106.2 %all_to_all.15 = f32[8,128,256,4]{2,3,0,1:T(4,128)} all-to-all(f32[8,128,256,4]{2,3,0,1:T(4,128)S(1)} %copy.14), channel_id=1, replica_groups=mesh['grp'=4,'dev'=64] {'dev'}, dimensions={1} | all-to-all | bytes 8388608 | tf_op jit(solution)/shard_map/all_to_all | solution.py:14
  116.9 50.4 %copy.15 = f32[8,64,2,256,4]{0,1,4,3,2:T(8,128)} copy(f32[8,64,2,256,4]{3,4,0,2,1:T(4,128)} %bitcast.63) | data formatting | bytes 8388608 | tf_op jit(solution)/shard_map/all_to_all | solution.py:14
  167.2 48.3 %reshape.21 = f32[512,2048]{0,1:T(8,128)} reshape(f32[64,8,2,256,4]{1,0,4,3,2:T(8,128)} %bitcast.1) | data formatting | bytes 8388608 | tf_op jit(solution)/shard_map/reshape | solution.py:17
  215.5 11.3 %fusion.17 = f32[512,512]{1,0:T(8,128)} fusion(f32[512,2048]{0,1:T(8,128)} %reshape.21), kind=kOutput, calls=%fused_computation.31 | convolution fusion | flops 6442450944 | bytes 5242880 | tf_op jit(solution)/shard_map/dot_general | solution.py:10
  226.9 0.0 all-reduce.2.cloned.1.call-update
  226.9 5.2 dot_general.36
  232.1 252.3 %all-reduce.2.cloned.1.call-done = f32[512,512]{1,0:T(8,128)} async-done(((f32[512,512]{1,0:T(8,128)}), f32[512,512]{1,0:T(8,128)}) %all-reduce.2.cloned.1.call-update) | async-done | bytes 1048592 | tf_op jit(solution)/shard_map/psum | solution.py:19
  484.4 0.0 copy-done
  484.4 0.0 copy-start.1
  484.4 2.4 fusion.18
  486.9 0.3 fusion.19
  487.2 0.1 copy.16
  487.2 5.8 %cholesky.59 = f32[64,64]{1,0:T(8,128)S(1)} custom-call(f32[64,64]{1,0:T(8,128)S(1)} %fusion.12), custom_call_target="Cholesky" | custom-call | tf_op jit(solution)/shard_map/jit(cholesky)/cholesky | solution.py:24
  493.1 0.6 compare_reduce_fusion.2
  493.8 0.7 fusion.3
  494.4 4.9 custom-call.7
  499.3 0.3 convolution_bitcast_fusion.1
  499.7 2.4 fusion.20
  502.0 0.3 fusion.21
  502.3 0.1 copy.17
  502.4 5.8 %cholesky.70 = f32[64,64]{1,0:T(8,128)S(1)} custom-call(f32[64,64]{1,0:T(8,128)S(1)} %fusion.10), custom_call_target="Cholesky" | custom-call | tf_op jit(solution)/shard_map/jit(cholesky)/cholesky | solution.py:24
  508.3 0.6 compare_reduce_fusion.1
  508.9 0.7 fusion.4
  509.6 4.9 custom-call.8
  514.5 0.3 convolution_bitcast_fusion
  514.8 0.0 copy-done.1
  514.8 1.1 fusion.22
  516.0 0.3 fusion.23
  516.2 0.1 copy.18
  516.3 5.8 %cholesky.81 = f32[64,64]{1,0:T(8,128)S(1)} custom-call(f32[64,64]{1,0:T(8,128)S(1)} %fusion.8), custom_call_target="Cholesky" | custom-call | tf_op jit(solution)/shard_map/jit(cholesky)/cholesky | solution.py:24
  522.2 0.6 compare_reduce_fusion
  522.9 0.7 fusion.5
  523.5 4.9 custom-call.9
  528.4 0.3 fusion.6
  528.8 0.0 copy-start.2
  528.8 7.1 %fusion = f32[64,2,256,4]{2,0,3,1:T(8,128)S(1)} fusion(f32[2,256,4,512]{3,2,1,0:T(4,128)} %dot_general.36, f32[64,512]{1,0:T(8,128)S(1)} %fusion.6), kind=kOutput, calls=%fused_computation | convolution fusion | flops 805306368 | bytes 4849664 | tf_op jit(solution)/shard_map/dot_general | solution.py:10
  535.9 1.1 copy.20
  537.0 0.0 copy-done.2
  (6 shorter events, 0.1 us)
Async XLA Ops:
  7.2 477.3 %copy-start = (f32[512,64]{0,1:T(8,128)S(1)}, f32[512,64]{0,1:T(8,128)}, u32[]{:S(2)}) copy-start(f32[512,64]{0,1:T(8,128)} %param.6) | copy-start | bytes 393220
  7.2 477.3 %all-reduce.2.cloned.1.call-start = ((), (), s32[]{:S(2)}) async-start(), calls=%async_computation.1 | async-start | bytes 2097152 | tf_op jit(solution)/shard_map/psum | solution.py:19
  484.4 30.4 %copy-start.1 = (f32[512,512]{1,0:T(8,128)S(1)}, f32[512,512]{1,0:T(8,128)}, u32[]{:S(2)}) copy-start(f32[512,512]{1,0:T(8,128)} %all-reduce.2.cloned.1.call-done) | copy-start | bytes 3145732
  528.8 8.3 %copy-start.2 = (f32[64,512]{1,0:T(8,128)}, f32[64,512]{1,0:T(8,128)S(1)}, u32[]{:S(2)}) copy-start(f32[64,512]{1,0:T(8,128)S(1)} %fusion.6) | copy-start | bytes 393220
Sparse Core Ops, SparseCore 0:
  227.0 257.3 all-reduce.1
where the time goes:
time: 545 us; the launch traced here: 544 us
  waiting for transfers between devices  252 us (46%)
  local copies, waits for them, and re-layouts  109 us (20%)
  blocking collectives  106 us (19%)
  other arithmetic  36.2 us (7%)
  matrix products  26.2 us (5%)
  between operations  14.2 us (3%)
    psum x1, waiting for transfers between devices, on_device(): gram = lax.psum(local_gram, ('grp', 'dev'))  252 us
    all_to_all x1, blocking collectives, on_device(): lax.all_to_all(field, 'dev', split_axis=1, concat_axis=0, tiled=True)  106 us
    all_to_all x1, local copies, waits for them, and re-layouts, on_device(): lax.all_to_all(field, 'dev', split_axis=1, concat_axis=0, tiled=True)  50.4 us
    reshape x1, local copies, waits for them, and re-layouts, on_device(): unfold = regrouped.reshape(rows, local_cols)  48.3 us
    dot_general x8, matrix products, product(): jnp.dot(left, right, precision=lax.Precision.HIGHEST, preferred_element_t...  25.2 us
    another operation x9, other arithmetic, on_device(): chol = jnp.linalg.cholesky(cross)  19.6 us
    another operation x6, other arithmetic, on_device(): lax.linalg.triangular_solve(chol, image, left_side=False, lower=True, tra...  16.6 us
  transfers between devices with their start and end apart: 1, of which 1 were waited for; matrix products, arithmetic and copies ran while one was open for 1% of the time, Pallas kernels for 0%

commit v1 on v0

--- a/solution.py
+++ b/solution.py
@@ -16,7 +16,9 @@
     local_cols = regrouped.shape[1] * regrouped.shape[2] * regrouped.shape[3]
     unfold = regrouped.reshape(rows, local_cols)
     local_gram = product(unfold, unfold.T)
-    gram = lax.psum(local_gram, ("grp", "dev"))
+    gram = local_gram
+    for over in ("grp", "dev"):
+        gram = lax.psum(gram, over)
     basis = start_basis
     for step in range(ITERS):
         image = product(gram, basis)

time: 545 us -> 529 us (0.971)
  waiting for transfers between devices: 252 us -> 236 us
    psum x1 -> x2, waiting for transfers between devices: 252 us -> 236 us  [on_device(): gram = lax.psum(gram, over)]
  transfers between devices with their start and end apart: 1 -> 2, of which waited for: 1 -> 2; matrix products, arithmetic and copies ran while one was open for 1% -> 1% of each run, Pallas kernels for 0% -> 0%
where the time goes in v1:
time: 529 us; the launch traced here: 527 us
  waiting for transfers between devices  236 us (45%)
  local copies, waits for them, and re-layouts  109 us (21%)
  blocking collectives  106 us (20%)
  other arithmetic  36.2 us (7%)
  matrix products  26.1 us (5%)
  between operations  14.2 us (3%)
    psum x2, waiting for transfers between devices, on_device(): gram = lax.psum(gram, over)  236 us
    all_to_all x1, blocking collectives, on_device(): lax.all_to_all(field, 'dev', split_axis=1, concat_axis=0, tiled=True)  106 us
    all_to_all x1, local copies, waits for them, and re-layouts, on_device(): lax.all_to_all(field, 'dev', split_axis=1, concat_axis=0, tiled=True)  50.4 us
    reshape x1, local copies, waits for them, and re-layouts, on_device(): unfold = regrouped.reshape(rows, local_cols)  48.3 us
    dot_general x8, matrix products, product(): jnp.dot(left, right, precision=lax.Precision.HIGHEST, preferred_element_t...  25.1 us
    another operation x9, other arithmetic, on_device(): chol = jnp.linalg.cholesky(cross)  19.6 us
    another operation x6, other arithmetic, on_device(): lax.linalg.triangular_solve(chol, image, left_side=False, lower=True, tra...  16.6 us
  transfers between devices with their start and end apart: 2, of which 2 were waited for; matrix products, arithmetic and copies ran while one was open for 1% of the time, Pallas kernels for 0%

profile of v1, /device:TPU:2, one launch (start us, length us, event | category | flops | bytes accessed | tf_op | source)
XLA Modules:
  0.0 527.5 jit_solution(3021086049878920090)
XLA Ops:
  7.2 0.0 copy-start
  7.2 0.0 all-reduce.3.cloned.1.call-start
  7.2 3.4 copy.14
  10.7 106.2 %all_to_all.15 = f32[8,128,256,4]{2,3,0,1:T(4,128)} all-to-all(f32[8,128,256,4]{2,3,0,1:T(4,128)S(1)} %copy.14), channel_id=1, replica_groups=mesh['grp'=4,'dev'=64] {'dev'}, dimensions={1} | all-to-all | bytes 8388608 | tf_op jit(solution)/shard_map/all_to_all | solution.py:14
  116.9 50.4 %copy.15 = f32[8,64,2,256,4]{0,1,4,3,2:T(8,128)} copy(f32[8,64,2,256,4]{3,4,0,2,1:T(4,128)} %bitcast.63) | data formatting | bytes 8388608 | tf_op jit(solution)/shard_map/all_to_all | solution.py:14
  167.2 48.3 %reshape.21 = f32[512,2048]{0,1:T(8,128)} reshape(f32[64,8,2,256,4]{1,0,4,3,2:T(8,128)} %bitcast.1) | data formatting | bytes 8388608 | tf_op jit(solution)/shard_map/reshape | solution.py:17
  215.5 11.3 %fusion.17 = f32[512,512]{1,0:T(8,128)} fusion(f32[512,2048]{0,1:T(8,128)} %reshape.21), kind=kOutput, calls=%fused_computation.31 | convolution fusion | flops 6442450944 | bytes 5242880 | tf_op jit(solution)/shard_map/dot_general | solution.py:10
  226.9 0.0 all-reduce.3.cloned.1.call-update
  226.9 0.0 all-reduce.5.cloned.1.call-start
  226.9 49.9 %all-reduce.3.cloned.1.call-done = f32[512,512]{1,0:T(8,128)} async-done(((f32[512,512]{1,0:T(8,128)}), f32[512,512]{1,0:T(8,128)}) %all-reduce.3.cloned.1.call-update) | async-done | bytes 1048592 | tf_op jit(solution)/shard_map/psum | solution.py:21
  276.8 0.0 all-reduce.5.cloned.1.call-update
  276.9 5.2 dot_general.36
  282.0 186.0 %all-reduce.5.cloned.1.call-done = f32[512,512]{1,0:T(8,128)} async-done(((f32[512,512]{1,0:T(8,128)}), f32[512,512]{1,0:T(8,128)}) %all-reduce.5.cloned.1.call-update) | async-done | bytes 1048592 | tf_op jit(solution)/shard_map/psum | solution.py:21
  468.1 0.0 copy-done
  468.1 0.0 copy-start.1
  468.1 2.4 fusion.18
  470.5 0.3 fusion.19
  470.8 0.1 copy.16
  470.9 5.8 %cholesky.59 = f32[64,64]{1,0:T(8,128)S(1)} custom-call(f32[64,64]{1,0:T(8,128)S(1)} %fusion.12), custom_call_target="Cholesky" | custom-call | tf_op jit(solution)/shard_map/jit(cholesky)/cholesky | solution.py:26
  476.8 0.6 compare_reduce_fusion.2
  477.4 0.7 fusion.3
  478.1 4.9 custom-call.7
  483.0 0.3 convolution_bitcast_fusion.1
  483.3 2.4 fusion.20
  485.7 0.3 fusion.21
  485.9 0.1 copy.17
  486.0 5.8 %cholesky.70 = f32[64,64]{1,0:T(8,128)S(1)} custom-call(f32[64,64]{1,0:T(8,128)S(1)} %fusion.10), custom_call_target="Cholesky" | custom-call | tf_op jit(solution)/shard_map/jit(cholesky)/cholesky | solution.py:26
  491.9 0.6 compare_reduce_fusion.1
  492.5 0.7 fusion.4
  493.2 4.9 custom-call.8
  498.1 0.3 convolution_bitcast_fusion
  498.4 0.0 copy-done.1
  498.5 1.1 fusion.22
  499.6 0.3 fusion.23
  499.9 0.1 copy.18
  500.0 5.8 %cholesky.81 = f32[64,64]{1,0:T(8,128)S(1)} custom-call(f32[64,64]{1,0:T(8,128)S(1)} %fusion.8), custom_call_target="Cholesky" | custom-call | tf_op jit(solution)/shard_map/jit(cholesky)/cholesky | solution.py:26
  505.8 0.6 compare_reduce_fusion
  506.5 0.7 fusion.5
  507.1 4.9 custom-call.9
  512.0 0.3 fusion.6
  512.4 0.0 copy-start.2
  512.4 7.1 %fusion = f32[64,2,256,4]{2,0,3,1:T(8,128)S(1)} fusion(f32[2,256,4,512]{3,2,1,0:T(4,128)} %dot_general.36, f32[64,512]{1,0:T(8,128)S(1)} %fusion.6), kind=kOutput, calls=%fused_computation | convolution fusion | flops 805306368 | bytes 4849664 | tf_op jit(solution)/shard_map/dot_general | solution.py:10
  519.5 1.1 copy.20
  520.6 0.0 copy-done.2
  (6 shorter events, 0.1 us)
Async XLA Ops:
  7.2 460.9 %copy-start = (f32[512,64]{0,1:T(8,128)S(1)}, f32[512,64]{0,1:T(8,128)}, u32[]{:S(2)}) copy-start(f32[512,64]{0,1:T(8,128)} %param.6) | copy-start | bytes 393220
  7.2 269.7 %all-reduce.3.cloned.1.call-start = ((), (), s32[]{:S(2)}) async-start(), calls=%async_computation.1 | async-start | bytes 2097152 | tf_op jit(solution)/shard_map/psum | solution.py:21
  226.9 241.2 %all-reduce.5.cloned.1.call-start = ((), (), s32[]{:S(2)}) async-start(), calls=%async_computation.2 | async-start | bytes 2097152 | tf_op jit(solution)/shard_map/psum | solution.py:21
  468.1 30.4 %copy-start.1 = (f32[512,512]{1,0:T(8,128)S(1)}, f32[512,512]{1,0:T(8,128)}, u32[]{:S(2)}) copy-start(f32[512,512]{1,0:T(8,128)} %all-reduce.5.cloned.1.call-done) | copy-start | bytes 3145732
  512.4 8.3 %copy-start.2 = (f32[64,512]{1,0:T(8,128)}, f32[64,512]{1,0:T(8,128)S(1)}, u32[]{:S(2)}) copy-start(f32[64,512]{1,0:T(8,128)S(1)} %fusion.6) | copy-start | bytes 393220
Sparse Core Ops, SparseCore 0:
  227.0 49.7 all-reduce.2
  280.3 187.7 all-reduce.4
